TPU v7x, 32 devices: a whole 2x2x4 slice. The times are simulated.
32 devices in a mesh: wide: 16 (over z, y, x), narrow: 2 (over core).
Axes of the slice: x: 2, y: 2, z: 4, core: 2. Of those that a mesh axis runs over, the one named last changes fastest.
Arguments:
- passages: bfloat16 [16384, 768], P('wide'), may hold values from -32 to 32
- centroids: bfloat16 [4096, 768], P('narrow'), may hold values from -6 to 6
Outputs:
- new_centroids: float32 [4096, 768], P('narrow')
- row_potential: float32 [16384], P('wide')
- col_potential: float32 [4096], P('narrow')
All inputs are finite; a program needn't handle non-finite values.
Results may differ from a plain program's by a relative error of at most 0.00035.
Values sent between devices are 32-bit elements; how exact they have to be, the bound alone decides.
A program may use at most 64 MiB of HBM per device.

v0:
```python
import jax
import jax.numpy as jnp
from jax import lax
from jax.sharding import PartitionSpec as P

VECTOR_DIMENSION = 768
CENTROIDS = 4096
SWEEPS = 3
entropic_regularizer = 0.02


def inverse_rms(values):
    wide_values = values.astype(jnp.float32)
    return lax.rsqrt(jnp.mean(wide_values * wide_values, axis=1) + 1e-06)


def unit_rows(totals):
    return totals * lax.rsqrt(jnp.mean(totals * totals, axis=1, keepdims=True) + 1e-06)


def body(passages, centroids):
    passage_row_scale = inverse_rms(passages)
    cluster_center_factor = inverse_rms(centroids)
    cosine_affinity_matrix = lax.dot_general(
        passages, centroids, (((1,), (1,)), ((), ())), preferred_element_type=jnp.float32
    )
    kernel = jnp.exp(
        cosine_affinity_matrix
        * passage_row_scale[:, None]
        * cluster_center_factor[None, :]
        * (1.0 / (VECTOR_DIMENSION * entropic_regularizer))
    )
    target = float(lax.axis_size("wide") * passages.shape[0]) / float(
        lax.axis_size("narrow") * centroids.shape[0]
    )
    col_factor = jnp.ones((centroids.shape[0],), jnp.float32)
    row_factor = jnp.ones((passages.shape[0],), jnp.float32)
    for number in range(SWEEPS):
        row_part = jnp.dot(kernel, col_factor, precision=lax.Precision.HIGHEST)
        row_factor = 1.0 / lax.psum(row_part, "narrow")
        col_part = jnp.dot(row_factor, kernel, precision=lax.Precision.HIGHEST)
        col_factor = target / lax.psum(col_part, "wide")
    weights = (
        row_factor[:, None] * kernel * col_factor[None, :] * passage_row_scale[:, None]
    ).astype(jnp.bfloat16)
    partial_sums = lax.dot_general(
        weights, passages, (((0,), (0,)), ((), ())), preferred_element_type=jnp.float32
    )
    new_centroids = unit_rows(lax.psum(partial_sums, "wide"))
    row_potential = jnp.log(CENTROIDS * row_factor)
    return (new_centroids, row_potential, jnp.log(col_factor))


def solution(mesh):
    in_specs = (P("wide", None), P("narrow", None))
    out_specs = (P("narrow", None), P("wide"), P("narrow"))
    return jax.shard_map(body, mesh=mesh, in_specs=in_specs, out_specs=out_specs, check_vma=False)
```

profile of v0, /device:TPU:0, one launch (start us, length us, event | category | flops | bytes accessed | tf_op | source)
XLA Modules:
  0.0 426.3 jit_solution(12740581471887425097)
XLA Ops:
  7.2 0.0 all-reduce.2.cloned.1.call-start
  7.2 1.8 multiply_reduce_fusion.2
  9.0 2.6 multiply_reduce_fusion.1
  11.6 6.0 %multiply_exponential_fusion = f32[1024,2048]{1,0:T(8,128)S(1)} fusion(bf16[1024,768]{1,0:T(8,128)(2,1)} %param.2, bf16[2048,768]{1,0:T(8,128)(2,1)} %param.3, f32[2048]{0:T(1024)S(1)} %add_rsqrt_fusion.1, f32[1024]{0:T(1024)S(1)} %add_rsqrt_fusion.2), kind=kOutput, calls=%fused_computation.1 | convolution fusion | flops 3227516928 | bytes 13119488 | tf_op jit(solution)/shard_map/dot_general | solution.py:24
  17.6 0.0 copy-start
  17.6 3.2 copy-done
  20.8 7.1 %fusion.4 = f32[1,1024]{1,0:T(1,128)S(1)} fusion(f32[1024,2048]{1,0:T(8,128)S(1)} %multiply_exponential_fusion), kind=kOutput, calls=%fused_computation.12 | convolution fusion | flops 25165824 | bytes 8392704 | tf_op jit(solution)/shard_map/dot_general | solution.py:39
  28.0 2.6 psum.49
  30.6 6.3 %fusion.8 = f32[1,2048]{1,0:T(1,128)S(1)} fusion(f32[1024,1]{0,1:T(1,128)S(1)} %bitcast.31, f32[1024,2048]{1,0:T(8,128)} %copy-done), kind=kOutput, calls=%fused_computation.24 | convolution fusion | flops 25165824 | bytes 8400896 | tf_op jit(solution)/shard_map/dot_general | solution.py:41
  36.9 44.0 %psum.50 = f32[2048]{0:T(1024)S(1)} all-reduce(f32[2048]{0:T(1024)S(1)} %bitcast.25), channel_id=1, replica_groups=mesh['wide'=16,'narrow'=2] {'wide'}, use_global_device_ids=true, to_apply=%region_3.0 | all-reduce | flops 2048 | bytes 16384 | tf_op jit(solution)/shard_map/psum | solution.py:42
  81.0 9.4 %fusion.9 = f32[1,1024]{1,0:T(1,128)S(1)} fusion(f32[1024,2048]{1,0:T(8,128)} %copy-done, f32[2048,1]{0,1:T(1,128)S(1)} %bitcast.26), kind=kOutput, calls=%fused_computation.25 | convolution fusion | flops 25165824 | bytes 8400896 | tf_op jit(solution)/shard_map/dot_general | solution.py:39
  90.4 2.5 psum.51
  92.9 6.3 %fusion.10 = f32[1,2048]{1,0:T(1,128)S(1)} fusion(f32[1024,1]{0,1:T(1,128)S(1)} %bitcast.33, f32[1024,2048]{1,0:T(8,128)} %copy-done), kind=kOutput, calls=%fused_computation.26 | convolution fusion | flops 25165824 | bytes 8400896 | tf_op jit(solution)/shard_map/dot_general | solution.py:41
  99.2 37.1 %psum.52 = f32[2048]{0:T(1024)S(1)} all-reduce(f32[2048]{0:T(1024)S(1)} %bitcast.27), channel_id=1, replica_groups=mesh['wide'=16,'narrow'=2] {'wide'}, use_global_device_ids=true, to_apply=%region_5.0 | all-reduce | flops 2048 | bytes 16384 | tf_op jit(solution)/shard_map/psum | solution.py:42
  136.3 0.0 copy-start.2
  136.3 9.5 %fusion.11 = f32[1,1024]{1,0:T(1,128)S(1)} fusion(f32[1024,2048]{1,0:T(8,128)} %copy-done, f32[2048,1]{0,1:T(1,128)S(1)} %bitcast.28), kind=kOutput, calls=%fused_computation.27 | convolution fusion | flops 25165824 | bytes 8400896 | tf_op jit(solution)/shard_map/dot_general | solution.py:39
  145.8 2.5 psum.53
  148.3 0.6 multiply_log_fusion
  148.9 6.3 %fusion.12 = f32[1,2048]{1,0:T(1,128)S(1)} fusion(f32[1024,1]{0,1:T(1,128)S(1)} %bitcast.30, f32[1024,2048]{1,0:T(8,128)} %copy-done), kind=kOutput, calls=%fused_computation.28 | convolution fusion | flops 25165824 | bytes 8400896 | tf_op jit(solution)/shard_map/dot_general | solution.py:41
  155.2 39.3 %psum.54 = f32[2048]{0:T(1024)S(1)} all-reduce(f32[2048]{0:T(1024)S(1)} %bitcast.29), channel_id=1, replica_groups=mesh['wide'=16,'narrow'=2] {'wide'}, use_global_device_ids=true, to_apply=%region_7.0 | all-reduce | flops 2048 | bytes 16384 | tf_op jit(solution)/shard_map/psum | solution.py:42
  194.6 0.6 fusion.7
  195.2 0.0 copy-done.2
  195.2 10.1 %fusion = f32[2048,768]{1,0:T(8,128)} fusion(bf16[1024,768]{1,0:T(8,128)(2,1)S(1)} %copy-done.2, f32[1024,2048]{1,0:T(8,128)} %copy-done, f32[2048]{0:T(1024)S(1)} %get-tuple-element.4, f32[1024]{0:T(1024)S(1)} %get-tuple-element.6, f32[1024]{0:T(1024)S(1)} %add_rsqrt_fusion.2), kind=kOutput, calls=%fused_computation.4 | convolution fusion | flops 3229614080 | bytes 16269312 | tf_op jit(solution)/shard_map/dot_general | solution.py:46
  205.3 0.0 all-reduce.2.cloned.1.call-update
  205.3 206.4 %all-reduce.2.cloned.1.call-done = f32[2048,768]{1,0:T(8,128)} async-done(((f32[2048,768]{1,0:T(8,128)}), f32[2048,768]{1,0:T(8,128)}) %all-reduce.2.cloned.1.call-update) | async-done | bytes 6291472 | tf_op jit(solution)/shard_map/psum | solution.py:49
  411.7 0.0 copy-start.1
  411.7 3.4 multiply_reduce_fusion
  415.1 1.2 copy-done.1
  416.3 3.2 broadcast_multiply_fusion
  (7 shorter events, 0.0 us)
Async XLA Ops:
  7.2 404.5 %all-reduce.2.cloned.1.call-start = ((), (), s32[]{:S(2)}) async-start(), calls=%async_computation | async-start | bytes 12582912 | tf_op jit(solution)/shard_map/psum | solution.py:49
  17.6 3.2 copy-start
  136.3 58.9 %copy-start.2 = (bf16[1024,768]{1,0:T(8,128)(2,1)S(1)}, bf16[1024,768]{1,0:T(8,128)(2,1)}, u32[]{:S(2)}) copy-start(bf16[1024,768]{1,0:T(8,128)(2,1)} %param.2) | copy-start | bytes 4718596
  411.7 4.6 %copy-start.1 = (f32[2048,768]{1,0:T(8,128)S(1)}, f32[2048,768]{1,0:T(8,128)}, u32[]{:S(2)}) copy-start(f32[2048,768]{1,0:T(8,128)} %all-reduce.2.cloned.1.call-done) | copy-start | bytes 18874372
Sparse Core Ops, SparseCore 0:
  205.4 206.2 all-reduce.1
where the time goes:
time: 427 us; the launch traced here: 426 us
  waiting for transfers between devices  206 us (48%)
  blocking collectives  128 us (30%)
  matrix products  61.2 us (14%)
  between operations  14.1 us (3%)
  other arithmetic  12.2 us (3%)
  local copies, waits for them, and re-layouts  4.39 us (1%)
    psum x1, waiting for transfers between devices, body(): new_centroids = unit_rows(lax.psum(partial_sums, 'wide'))  206 us
    psum x3, blocking collectives, body(): col_factor = target / lax.psum(col_part, 'wide')  120 us
    dot_general x3, matrix products, body(): row_part = jnp.dot(kernel, col_factor, precision=lax.Precision.HIGHEST)  26 us
    dot_general x3, matrix products, body(): col_part = jnp.dot(row_factor, kernel, precision=lax.Precision.HIGHEST)  19 us
    dot_general x1, matrix products, body(): lax.dot_general(weights, passages, (((0,), (0,)), ((), ())), preferred_el...  10.1 us
  transfers between devices with their start and end apart: 1, of which 1 were waited for; matrix products, arithmetic and copies ran while one was open for 0% of the time, Pallas kernels for 0%

commit v1 on v0

--- a/solution.py
+++ b/solution.py
@@ -7,6 +7,10 @@
 CENTROIDS = 4096
 SWEEPS = 3
 entropic_regularizer = 0.02
+
+
+def touch_plate_in(z_in, bus_axis):
+    return jnp.sum(lax.all_gather(z_in, bus_axis), axis=0)
 
 
 def inverse_rms(values):
@@ -39,7 +43,7 @@
         row_part = jnp.dot(kernel, col_factor, precision=lax.Precision.HIGHEST)
         row_factor = 1.0 / lax.psum(row_part, "narrow")
         col_part = jnp.dot(row_factor, kernel, precision=lax.Precision.HIGHEST)
-        col_factor = target / lax.psum(col_part, "wide")
+        col_factor = target / touch_plate_in(col_part, "wide")
     weights = (
         row_factor[:, None] * kernel * col_factor[None, :] * passage_row_scale[:, None]
     ).astype(jnp.bfloat16)

time: 427 us -> 424 us (level)
    psum x3 -> x0, blocking collectives: 120 us -> none  [body(): col_factor = target / lax.psum(col_part, 'wide')]
    all_gather x0 -> x3, blocking collectives: none -> 118 us  [touch_plate_in(): return jnp.sum(lax.all_gather(z_in, bus_axis), axis=0)]
where the time goes in v1:
time: 424 us
  waiting for transfers between devices  206 us (49%)
  blocking collectives  125 us (29%)
  matrix products  61.2 us (14%)
  between operations  14.1 us (3%)
  other arithmetic  12.3 us (3%)
  local copies, waits for them, and re-layouts  4.47 us (1%)
    psum x1, waiting for transfers between devices, body(): new_centroids = unit_rows(lax.psum(partial_sums, 'wide'))  206 us
    all_gather x3, blocking collectives, touch_plate_in(): return jnp.sum(lax.all_gather(z_in, bus_axis), axis=0)  118 us
    dot_general x3, matrix products, body(): row_part = jnp.dot(kernel, col_factor, precision=lax.Precision.HIGHEST)  26 us
    dot_general x3, matrix products, body(): col_part = jnp.dot(row_factor, kernel, precision=lax.Precision.HIGHEST)  19 us
    dot_general x1, matrix products, body(): lax.dot_general(weights, passages, (((0,), (0,)), ((), ())), preferred_el...  10.1 us
  transfers between devices with their start and end apart: 1, of which 1 were waited for; matrix products, arithmetic and copies ran while one was open for 0% of the time, Pallas kernels for 0%

profile of v1, /device:TPU:0, one launch (start us, length us, event | category | flops | bytes accessed | tf_op | source)
XLA Modules:
  0.0 423.6 jit_solution(8781552148967216192)
XLA Ops:
  7.2 0.0 all-reduce.2.cloned.1.call-start
  7.2 1.8 multiply_reduce_fusion.2
  9.0 2.6 multiply_reduce_fusion.1
  11.6 6.0 %multiply_exponential_fusion = f32[1024,2048]{1,0:T(8,128)S(1)} fusion(bf16[1024,768]{1,0:T(8,128)(2,1)} %param.2, bf16[2048,768]{1,0:T(8,128)(2,1)} %param.3, f32[2048]{0:T(1024)S(1)} %add_rsqrt_fusion.1, f32[1024]{0:T(1024)S(1)} %add_rsqrt_fusion.2), kind=kOutput, calls=%fused_computation.1 | convolution fusion | flops 3227516928 | bytes 13119488 | tf_op jit(solution)/shard_map/dot_general | solution.py:28
  17.6 0.0 copy-start
  17.6 3.2 copy-done
  20.8 7.1 %fusion.4 = f32[1,1024]{1,0:T(1,128)S(1)} fusion(f32[1024,2048]{1,0:T(8,128)S(1)} %multiply_exponential_fusion), kind=kOutput, calls=%fused_computation.12 | convolution fusion | flops 25165824 | bytes 8392704 | tf_op jit(solution)/shard_map/dot_general | solution.py:43
  28.0 2.6 psum.28
  30.6 6.3 %fusion.8 = f32[1,2048]{1,0:T(1,128)S(1)} fusion(f32[1024,1]{0,1:T(1,128)S(1)} %bitcast.31, f32[1024,2048]{1,0:T(8,128)} %copy-done), kind=kOutput, calls=%fused_computation.24 | convolution fusion | flops 25165824 | bytes 8400896 | tf_op jit(solution)/shard_map/dot_general | solution.py:45
  36.9 43.1 %all-gather = f32[32768]{0:T(1024)S(1)} all-gather(f32[2048]{0:T(1024)S(1)} %bitcast.25), channel_id=2, replica_groups=mesh['wide'=16,'narrow'=2] {'wide'}, dimensions={0}, use_global_device_ids=true | all-gather | bytes 139264 | tf_op jit(solution)/shard_map/all_gather | solution.py:13
  80.1 9.4 %fusion.9 = f32[1,1024]{1,0:T(1,128)S(1)} fusion(f32[1024,2048]{1,0:T(8,128)} %copy-done, f32[2048,1]{0,1:T(1,128)S(1)} %bitcast.28), kind=kOutput, calls=%fused_computation.25 | convolution fusion | flops 25165824 | bytes 8400896 | tf_op jit(solution)/shard_map/dot_general | solution.py:43
  89.5 2.5 psum.29
  92.0 6.3 %fusion.10 = f32[1,2048]{1,0:T(1,128)S(1)} fusion(f32[1024,1]{0,1:T(1,128)S(1)} %bitcast.33, f32[1024,2048]{1,0:T(8,128)} %copy-done), kind=kOutput, calls=%fused_computation.26 | convolution fusion | flops 25165824 | bytes 8400896 | tf_op jit(solution)/shard_map/dot_general | solution.py:45
  98.4 36.1 %all-gather.1 = f32[32768]{0:T(1024)S(1)} all-gather(f32[2048]{0:T(1024)S(1)} %bitcast.26), channel_id=3, replica_groups=mesh['wide'=16,'narrow'=2] {'wide'}, dimensions={0}, use_global_device_ids=true | all-gather | bytes 139264 | tf_op jit(solution)/shard_map/all_gather | solution.py:13
  134.6 0.0 copy-start.2
  134.6 9.5 %fusion.11 = f32[1,1024]{1,0:T(1,128)S(1)} fusion(f32[1024,2048]{1,0:T(8,128)} %copy-done, f32[2048,1]{0,1:T(1,128)S(1)} %bitcast.29), kind=kOutput, calls=%fused_computation.27 | convolution fusion | flops 25165824 | bytes 8400896 | tf_op jit(solution)/shard_map/dot_general | solution.py:43
  144.1 2.5 psum.30
  146.6 0.6 multiply_log_fusion
  147.2 6.3 %fusion.12 = f32[1,2048]{1,0:T(1,128)S(1)} fusion(f32[1024,1]{0,1:T(1,128)S(1)} %bitcast.30, f32[1024,2048]{1,0:T(8,128)} %copy-done), kind=kOutput, calls=%fused_computation.28 | convolution fusion | flops 25165824 | bytes 8400896 | tf_op jit(solution)/shard_map/dot_general | solution.py:45
  153.5 38.4 %all-gather.2 = f32[32768]{0:T(1024)S(1)} all-gather(f32[2048]{0:T(1024)S(1)} %bitcast.27), channel_id=4, replica_groups=mesh['wide'=16,'narrow'=2] {'wide'}, dimensions={0}, use_global_device_ids=true | all-gather | bytes 139264 | tf_op jit(solution)/shard_map/all_gather | solution.py:13
  191.9 0.6 fusion.7
  192.6 0.0 copy-done.2
  192.6 10.1 %fusion = f32[2048,768]{1,0:T(8,128)} fusion(bf16[1024,768]{1,0:T(8,128)(2,1)S(1)} %copy-done.2, f32[1024,2048]{1,0:T(8,128)} %copy-done, f32[2048]{0:T(1024)S(1)} %get-tuple-element.4, f32[1024]{0:T(1024)S(1)} %get-tuple-element.6, f32[1024]{0:T(1024)S(1)} %add_rsqrt_fusion.2), kind=kOutput, calls=%fused_computation.4 | convolution fusion | flops 3229614080 | bytes 16269312 | tf_op jit(solution)/shard_map/dot_general | solution.py:50
  202.7 0.0 all-reduce.2.cloned.1.call-update
  202.7 206.3 %all-reduce.2.cloned.1.call-done = f32[2048,768]{1,0:T(8,128)} async-done(((f32[2048,768]{1,0:T(8,128)}), f32[2048,768]{1,0:T(8,128)}) %all-reduce.2.cloned.1.call-update) | async-done | bytes 6291472 | tf_op jit(solution)/shard_map/psum | solution.py:53
  409.0 0.0 copy-start.1
  409.0 3.4 multiply_reduce_fusion
  412.4 1.2 copy-done.1
  413.6 3.2 broadcast_multiply_fusion
  (13 shorter events, 0.2 us)
Async XLA Ops:
  7.2 401.8 %all-reduce.2.cloned.1.call-start = ((), (), s32[]{:S(2)}) async-start(), calls=%async_computation | async-start | bytes 12582912 | tf_op jit(solution)/shard_map/psum | solution.py:53
  17.6 3.2 copy-start
  134.6 58.0 %copy-start.2 = (bf16[1024,768]{1,0:T(8,128)(2,1)S(1)}, bf16[1024,768]{1,0:T(8,128)(2,1)}, u32[]{:S(2)}) copy-start(bf16[1024,768]{1,0:T(8,128)(2,1)} %param.2) | copy-start | bytes 4718596
  409.0 4.6 %copy-start.1 = (f32[2048,768]{1,0:T(8,128)S(1)}, f32[2048,768]{1,0:T(8,128)}, u32[]{:S(2)}) copy-start(f32[2048,768]{1,0:T(8,128)} %all-reduce.2.cloned.1.call-done) | copy-start | bytes 18874372
Sparse Core Ops, SparseCore 0:
  202.8 206.1 all-reduce.1
